TPU v7x, 256 devices: a whole 4x4x8 slice. The times are simulated.
256 devices in a mesh: owner: 16 (over y, z_lo, core), dp: 16 (over z_hi, x).
Axes of the slice: x: 4, y: 4, z: 8 (z_hi: 4, z_lo: 2; z = z_hi * 2 + z_lo), core: 2. Of those that a mesh axis runs over, the one named last changes fastest.
Arguments:
- activations: bfloat16 [512, 8, 8, 512], P(('owner', 'dp')), may hold values from -8 to 8
- out_grad: bfloat16 [512, 8, 8, 512], P(('owner', 'dp')), may hold values from -6 to 6
- group_weight: bfloat16 [16, 288, 32], replicated, may hold values from -0.375 to 0.375
- proj_weight: bfloat16 [512, 512], replicated, may hold values from -0.25 to 0.25
- bn_gain: float32 [512], replicated, may hold values from 0.1 to 1.9
- bn_shift: float32 [512], replicated, may hold values from -3 to 3
- slot_block: int32 [16, 6], replicated, may hold values from -1 to 47, as said below
Outputs:
- group_grad: float32 [16, 288, 32], replicated
- proj_grad: float32 [512, 512], replicated
- out_factor: float32 [16, 32, 32], replicated
- factor_owned: float32 [96, 96, 288], P('owner', 'dp')
Inputs may be any that keep to these rules, and one draw needn't show every extreme that they name: `slot_block`: each of the 48 blocks stands in exactly one slot; an owner's blocks fill its slots from the first, the rest hold -1; some owner's 6 slots are all used.
All inputs are finite; a program needn't handle non-finite values.
Results may differ from a plain program's by a relative error of at most 0.0065.
Values sent between devices are 32-bit elements; how exact they have to be, the bound alone decides.
A program may use at most 64 MiB of HBM per device.

v0:
```python
import math

import jax
import jax.numpy as jnp
from jax import lax
from jax.sharding import PartitionSpec as P


def pick_slots(factor_blocks, slot_block):
    flat_slots = slot_block.reshape(-1)
    picked = jnp.take(factor_blocks, jnp.clip(flat_slots, 0, factor_blocks.shape[0] - 1), axis=0)
    return picked * (flat_slots >= 0).astype(jnp.float32)[:, None, None]


def per_device(activations, out_grad, group_weight, proj_weight, bn_gain, bn_shift, slot_block):
    img_count, side_len = (activations.shape[0], activations.shape[1])
    in_width = activations.shape[3]
    groups, patch_len, group_width = group_weight.shape
    out_width = out_grad.shape[3]
    row_count = img_count * side_len * side_len
    padded = jnp.pad(activations, ((0, 0), (1, 1), (1, 1), (0, 0)))
    padded = padded.reshape(img_count, side_len + 2, side_len + 2, groups, group_width)
    shifted = [
        padded[:, row_shift : row_shift + side_len, col_shift : col_shift + side_len]
        for row_shift in range(3)
        for col_shift in range(3)
    ]
    patches = jnp.stack(shifted, axis=4).reshape(row_count, groups, patch_len)
    conv_out = jnp.einsum(
        "rgp,gpo->rgo", patches, group_weight, preferred_element_type=jnp.float32
    ).reshape(row_count, in_width)
    preact = conv_out * bn_gain + bn_shift
    hidden = jnp.maximum(preact, 0.0).astype(jnp.bfloat16)
    upstream = out_grad.reshape(row_count, out_width)
    back_grad = jnp.einsum("ro,co->rc", upstream, proj_weight, preferred_element_type=jnp.float32)
    grad_pre = (
        jnp.where(preact > 0.0, back_grad * bn_gain, 0.0)
        .astype(jnp.bfloat16)
        .reshape(row_count, groups, group_width)
    )
    proj_part = jnp.einsum("rc,ro->co", hidden, upstream, preferred_element_type=jnp.float32)
    group_part = jnp.einsum("rgp,rgo->gpo", patches, grad_pre, preferred_element_type=jnp.float32)
    out_part = jnp.einsum("rga,rgb->gab", grad_pre, grad_pre, preferred_element_type=jnp.float32)
    in_part = jnp.einsum("rgp,rgq->gpq", patches, patches, preferred_element_type=jnp.float32)
    total_rows = row_count * lax.axis_size("owner") * lax.axis_size("dp")
    grad_scale = 1.0 / math.sqrt(total_rows)
    mean_scale = 1.0 / total_rows
    group_sum, proj_sum, out_sum = lax.psum((group_part, proj_part, out_part), ("owner", "dp"))
    factor_blocks = in_part.reshape(groups * 3, patch_len // 3, patch_len)
    slotted = pick_slots(factor_blocks, slot_block)
    owned = lax.psum_scatter(slotted, "owner", scatter_dimension=0, tiled=True)
    owned = lax.psum_scatter(owned, "dp", scatter_dimension=1, tiled=True)
    return (group_sum * grad_scale, proj_sum * grad_scale, out_sum * mean_scale, owned * mean_scale)


def solution(mesh):
    placed = (
        P(("owner", "dp"), None, None, None),
        P(("owner", "dp"), None, None, None),
        P(),
        P(),
        P(),
        P(),
        P(),
    )
    return jax.shard_map(
        per_device,
        mesh=mesh,
        in_specs=placed,
        out_specs=(P(), P(), P(), P("owner", "dp", None)),
        check_vma=False,
    )
```

profile of v0, /device:TPU:1, one launch (start us, length us, event | category | flops | bytes accessed | tf_op | source)
XLA Modules:
  0.0 602.3 jit_solution(6880874112571848941)
XLA Ops:
  8.1 0.7 broadcast_clamp_fusion
  9.1 0.7 compare_convert_fusion
  9.8 1.0 pad.4
  10.7 0.5 reshape.79
  12.0 11.1 %copy.54 = bf16[2,8,8,16,9,32]{5,4,3,2,1,0:T(8,128)(2,1)} copy(bf16[2,8,8,16,9,32]{5,3,2,1,0,4:T(8,128)(2,1)S(1)} %fusion.2) | data formatting | bytes 2359296 | tf_op jit(solution)/shard_map/stack | solution.py:28
  23.2 8.8 %reshape.80 = bf16[128,16,288]{2,1,0:T(8,128)(2,1)S(1)} reshape(bf16[2,8,8,16,9,32]{5,4,3,2,1,0:T(8,128)(2,1)} %copy.54) | data formatting | bytes 2359296 | tf_op jit(solution)/shard_map/reshape | solution.py:28
  32.0 1.1 copy.58
  33.0 3.9 fusion.18
  37.1 12.4 %gather_fusion = f32[96,96,288]{2,1,0:T(8,128)} fusion(f32[48,96,288]{2,1,0:T(8,128)} %bitcast.67, s32[1024]{0:T(1024)S(1)} %pad_clamp_fusion), kind=kCustom, calls=%fused_computation | custom fusion | bytes 21234048 | tf_op jit(solution)/shard_map/jit(_take)/gather | solution.py:11
  49.5 13.0 %select_multiply_fusion = f32[96,96,288]{2,1,0:T(8,128)} fusion(f32[96,96,288]{2,1,0:T(8,128)} %gather_fusion, f32[96]{0:T(128)S(1)} %reshape.85, pred[96]{0:T(512)(128)(4,1)S(1)} %compare_and_fusion), kind=kLoop, calls=%fused_computation.1 | loop fusion | flops 5308416 | bytes 21234144 | tf_op jit(solution)/shard_map/mul | solution.py:12
  62.6 0.6 copy-done.3
  63.5 0.4 fusion.13
  64.1 0.3 fusion.1
  64.5 0.9 fusion.17
  65.4 1.3 fusion.16
  66.7 1.4 fusion.15
  68.1 0.6 dynamic-slice
  69.4 158.6 %reduce-scatter.3.cloned.1.call-done = f32[6,96,288]{2,1,0:T(8,128)} async-done(((f32[96,96,288]{2,1,0:T(8,128)}), f32[6,96,288]{2,1,0:T(8,128)}) %reduce-scatter.3.cloned.1.call-update) | async-done | bytes 663568 | tf_op jit(solution)/shard_map/reduce_scatter | solution.py:51
  228.0 204.5 %all-reduce.8.cloned.1.call-done = (f32[16,288,32]{1,2,0:T(8,128)}, f32[512,512]{1,0:T(8,128)}, f32[16,32,32]{2,1,0:T(8,128)}) async-done(((f32[16,288,32]{1,2,0:T(8,128)}, f32[512,512]{1,0:T(8,128)}, f32[16,32,32]{2,1,0:T(8,128)}), (f32[16,288,32]{1,2,0:T(8,128)}, f32[512,512]{1,0:T(8,128)}, f32[16,32,32]{2,1,0:T(8,128)})) %all-reduce.8.cloned.1.call-update) | async-done | bytes 1703952 | tf_op jit(solution)/shard_map/psum | solution.py:48
  432.5 1.7 broadcast_multiply_fusion.2
  434.2 2.1 broadcast_multiply_fusion.1
  436.3 2.3 broadcast_multiply_fusion
  438.6 154.7 %all-reduce.6.cloned.1.call-done = f32[6,96,288]{2,1,0:T(8,128)} async-done(((f32[6,96,288]{2,1,0:T(8,128)}), f32[6,96,288]{2,1,0:T(8,128)}) %all-reduce.6.cloned.1.call-update) | async-done | bytes 663568
  593.3 1.6 dynamic-slice_multiply_fusion
  (38 shorter events, 2.0 us)
Async XLA Ops:
  8.0 56.1 %copy-start = (bf16[512,512]{1,0:T(8,128)(2,1)S(1)}, bf16[512,512]{1,0:T(8,128)(2,1)}, u32[]{:S(2)}) copy-start(bf16[512,512]{1,0:T(8,128)(2,1)} %param.10) | copy-start | bytes 1572868
  8.0 220.0 %reduce-scatter.3.cloned.1.call-start = ((), (), s32[]{:S(2)}) async-start(), calls=%async_computation.1 | async-start | bytes 15040512 | tf_op jit(solution)/shard_map/reduce_scatter | solution.py:51
  62.5 0.7 copy-start.3
  62.5 0.8 copy-start.4
  62.5 1.0 copy-start.2
  62.5 1.6 copy-start.1
  62.5 370.0 %all-reduce.8.cloned.1.call-start = ((), (), s32[]{:S(2)}) async-start(), calls=%async_computation.3 | async-start | bytes 4194304 | tf_op jit(solution)/shard_map/psum | solution.py:48
  63.5 4.6 copy-start.5
  68.1 525.2 %all-reduce.6.cloned.1.call-start = ((), (), s32[]{:S(2)}) async-start(), calls=%async_computation.2 | async-start | bytes 1769472
Sparse Core Ops, SparseCore 0:
  62.7 165.3 reduce-scatter.2
Sparse Core Ops, SparseCore 1:
  69.3 363.2 all-reduce.7
  435.0 158.2 all-reduce.5
where the time goes:
time: 613 us; the launch traced here: 602 us
  waiting for transfers between devices  518 us (85%)
  local copies, waits for them, and re-layouts  37.9 us (6%)
  other arithmetic  22 us (4%)
  between operations  16.3 us (3%)
  matrix products  8.09 us (1%)
    psum x1, waiting for transfers between devices, per_device(): lax.psum((group_part, proj_part, out_part), ('owner', 'dp'))  204 us
    reduce_scatter x1, waiting for transfers between devices, per_device(): owned = lax.psum_scatter(slotted, 'owner', scatter_dimension=0, tiled=True)  159 us
    unnamed x4, waiting for transfers between devices  155 us
    mul x1, other arithmetic, pick_slots(): return picked * (flat_slots >= 0).astype(jnp.float32)[:, None, None]  13 us
    gather x1, local copies, waits for them, and re-layouts, pick_slots(): jnp.take(factor_blocks, jnp.clip(flat_slots, 0, factor_blocks.shape[0] -...  12.4 us
  transfers between devices with their start and end apart: 3, of which 3 were waited for; matrix products, arithmetic and copies ran while one was open for 2% of the time, Pallas kernels for 0%

commit v1 on v0

v1 whole, which is shorter than its diff:
```python
import functools
import math

import jax
import jax.numpy as jnp
from jax import lax
from jax.experimental import pallas as pl
from jax.experimental.pallas import tpu as pltpu
from jax.sharding import PartitionSpec as P

MESH = pl.DeviceIdType.MESH
F32 = jnp.float32
BF16 = jnp.bfloat16
NT = (((1,), (1,)), ((), ()))
GROUPS, GW, CP = 16, 32, 288
N_OWNER, N_DP = 16, 16


def shifted_rows(tile, lane, store):
    row = (lane // 8) % 8
    col = lane % 8
    for a in range(3):
        for b in range(3):
            offset = (a - 1) * 8 + (b - 1)
            moved = tile if offset == 0 else pltpu.roll(tile, (-offset) % 128, 1)
            keep = None
            if a == 0:
                keep = row >= 1
            if a == 2:
                keep = row <= 6
            if b == 0:
                keep = (col >= 1) if keep is None else keep & (col >= 1)
            if b == 2:
                keep = (col <= 6) if keep is None else keep & (col <= 6)
            if keep is not None:
                moved = jnp.where(keep, moved, 0.0)
            store(3 * a + b, moved.astype(BF16))


def kernel(
    grad_scale, mean_scale,
    slot_ref, x_ref, u_ref, gw_ref, pw_ref, gain_ref, shift_ref,
    group_out, proj_out, outf_out, fact_out,
    x_t, g_t, rx, rg, pt, zt, gram, ppart, rcore, pacc, rpx, rpy, rpz,
    fg_send, rfg, zh_send, rzh, gfull, ffull,
    barrier_free,
    sx, rxs, sg, rgs, s_core, r_core, s_px, r_px, s_py, r_py, s_pz, r_pz,
    s_fg, r_fg, s_zh, r_zh,
    s_ga, r_ga, s_fa, r_fa, s_pa, r_pa,
):
    del barrier_free
    owner = lax.axis_index("owner")
    dp = lax.axis_index("dp")
    core = owner % 2
    zlo = (owner // 2) % 2
    y = owner // 4
    x = dp % 4
    zhi = dp // 4
    z = zhi * 2 + zlo

    def at_y(j):
        return (((y + j) % 4) * 4 + zlo * 2 + core, dp)

    def at_x(j):
        return (owner, zhi * 4 + (x + j) % 4)

    def at_z(j):
        there = (z + j) % 8
        return (y * 4 + (there % 2) * 2 + core, (there // 2) * 4 + x)

    def at_zhi(j):
        return (owner, ((zhi + j) % 4) * 4 + x)

    at_zlo = (y * 4 + (1 - zlo) * 2 + core, dp)
    at_core = (y * 4 + zlo * 2 + (1 - core), dp)

    def copy(src, dst, send, recv, device):
        return pltpu.make_async_remote_copy(
            src_ref=src, dst_ref=dst, send_sem=send, recv_sem=recv, device_id=device, device_id_type=MESH
        )

    barrier = pltpu.get_barrier_semaphore()
    for j in range(1, N_OWNER):
        pl.semaphore_signal(barrier, inc=1, device_id=((owner + j) % N_OWNER, dp), device_id_type=MESH)
    for j in range(1, 4):
        pl.semaphore_signal(barrier, inc=1, device_id=at_x(j), device_id_type=MESH)
    for j in range(1, 8):
        pl.semaphore_signal(barrier, inc=1, device_id=at_z(j), device_id_type=MESH)

    x_rows = x_ref[...].astype(F32).T
    x_t[...] = x_rows.reshape(GROUPS, GW, 128)
    pl.semaphore_wait(barrier, 25)

    def x_copy(j):
        there = (owner + j) % N_OWNER
        return copy(x_t.at[there], rx.at[owner], sx.at[j], rxs.at[owner], (there, dp))

    def g_copy(j):
        there = (owner + j) % N_OWNER
        return copy(g_t.at[there], rg.at[owner], sg.at[j], rgs.at[owner], (there, dp))

    def send_x(j, carry):
        x_copy(j).start()
        return carry

    lax.fori_loop(1, N_OWNER, send_x, 0)

    lane = lax.broadcasted_iota(jnp.int32, (GW, 128), 1)
    gain_col = jnp.broadcast_to(gain_ref[...], (128, 512)).T
    shift_col = jnp.broadcast_to(shift_ref[...], (128, 512)).T
    conv = []
    for g in range(GROUPS):
        def put(s, value, g=g):
            pt[g, s * GW:(s + 1) * GW, :] = value

        shifted_rows(x_rows[g * GW:(g + 1) * GW, :], lane, put)
        weight_t = gw_ref[g].astype(F32).T.astype(BF16)
        conv.append(jnp.dot(weight_t, pt[g], preferred_element_type=F32))
    preact = jnp.concatenate(conv, axis=0) * gain_col + shift_col
    upstream = u_ref[...]
    back = lax.dot_general(pw_ref[...], upstream, NT, preferred_element_type=F32)
    grad = jnp.where(preact > 0.0, back * gain_col, 0.0).astype(BF16).astype(F32)
    g_t[...] = grad.reshape(GROUPS, GW, 128)

    def send_g(j, carry):
        g_copy(j).start()
        return carry

    lax.fori_loop(1, N_OWNER, send_g, 0)

    hidden = jnp.maximum(preact, 0.0).astype(BF16)
    ppart[...] = jnp.dot(hidden, upstream, preferred_element_type=F32)
    far = pl.multiple_of((1 - core) * 256, 256)
    near = pl.multiple_of(core * 256, 256)
    core_copy = copy(ppart.at[pl.ds(far, 256)], rcore, s_core, r_core, at_core)
    core_copy.start()

    rx[owner] = x_t[owner]
    rg[owner] = g_t[owner]

    core_copy.wait_recv()
    pacc[...] = ppart[pl.ds(near, 256), :] + rcore[...]
    px_copies = []
    for j in range(1, 4):
        rows = pl.ds(pl.multiple_of(((x + j) % 4) * 64, 64), 64)
        px_copies.append(copy(pacc.at[rows], rpx.at[x], s_px.at[j], r_px.at[x], at_x(j)))
        px_copies[-1].start()

    def wait_in(ref, sems, slot, send):
        copy(ref, ref, send, sems.at[slot], at_core).wait_recv()

    zt[320:384, :] = jnp.zeros((64, 2048), BF16)
    for j in range(N_OWNER):
        source = (owner + j) % N_OWNER
        if j:
            wait_in(rx.at[source], rxs, source, sx.at[0])
        lanes = slice(j * 128, (j + 1) * 128)

        def put_z(s, value, lanes=lanes):
            zt[s * GW:(s + 1) * GW, lanes] = value

        shifted_rows(rx[source], lane, put_z)
    for j in range(N_OWNER):
        source = (owner + j) % N_OWNER
        if j:
            wait_in(rg.at[source], rgs, source, sg.at[0])
        zt[CP:CP + GW, j * 128:(j + 1) * 128] = rg[source].astype(BF16)
    gram[...] = lax.dot_general(zt[0:320, :], zt[...], NT, preferred_element_type=F32)

    for xx in range(4):
        for zz in range(4):
            for a in range(3):
                at = a * 96 + (zz * 4 + xx) * 6
                fg_send[xx, zz * 3 + a] = gram[at:at + 8, :]
        fg_send[xx, 12] = gram[CP + xx * 8:CP + xx * 8 + 8, :]
    fg_copies = []
    for j in range(1, 4):
        fg_copies.append(copy(fg_send.at[(x + j) % 4], rfg.at[x], s_fg.at[j], r_fg.at[x], at_x(j)))
        fg_copies[-1].start()

    own = pacc[pl.ds(pl.multiple_of(x * 64, 64), 64), :]
    for j in range(1, 4):
        slot = (x + j) % 4
        wait_in(rpx.at[slot], r_px, slot, s_px.at[0])
        own = own + rpx[slot]
    for copied in px_copies:
        copied.wait_send()
    pacc[0:64, :] = own
    py_copies = []
    for j in range(1, 4):
        rows = pl.ds(pl.multiple_of(((y + j) % 4) * 16, 16), 16)
        py_copies.append(copy(pacc.at[rows], rpy.at[y], s_py.at[j], r_py.at[y], at_y(j)))
        py_copies[-1].start()

    for j in range(1, 4):
        slot = (x + j) % 4
        wait_in(rfg.at[slot], r_fg, slot, s_fg.at[0])
    rfg[x] = fg_send[x]
    summed = (rfg[0] + rfg[1]) + (rfg[2] + rfg[3])
    for zz in range(4):
        zh_send[zz, 0:3] = summed[zz * 3:zz * 3 + 3]
        zh_send[zz, 3] = summed[12]
    zh_copies = []
    for j in range(1, 4):
        there = (zhi + j) % 4
        zh_copies.append(copy(zh_send.at[there], rzh.at[zhi], s_zh.at[j], r_zh.at[zhi], at_zhi(j)))
        zh_copies[-1].start()

    own = pacc[pl.ds(pl.multiple_of(y * 16, 16), 16), :]
    for j in range(1, 4):
        slot = (y + j) % 4
        wait_in(rpy.at[slot], r_py, slot, s_py.at[0])
        own = own + rpy[slot]
    for copied in py_copies:
        copied.wait_send()
    pacc[64:80, :] = own
    pz_copies = []

    def tile_of(there, base):
        return (
            pl.ds(pl.multiple_of(base + 8 * (there // 4), 8), 8),
            pl.ds(pl.multiple_of(128 * (there % 4), 128), 128),
        )

    for j in range(1, 8):
        there = (z + j) % 8
        pz_copies.append(copy(pacc.at[tile_of(there, 64)], rpz.at[z], s_pz.at[j], r_pz.at[z], at_z(j)))
        pz_copies[-1].start()

    for j in range(1, 4):
        slot = (zhi + j) % 4
        wait_in(rzh.at[slot], r_zh, slot, s_zh.at[0])
    rzh[zhi] = zh_send[zhi]
    summed = (rzh[0] + rzh[1]) + (rzh[2] + rzh[3])
    place = core * 8 + y * 2 + zlo
    ffull[place] = summed[0:3] * mean_scale
    wide = lax.broadcasted_iota(jnp.int32, (8, 384), 1)
    row8 = pl.ds(pl.multiple_of(x * 8, 8), 8)
    gfull[place, row8, :] = summed[3] * jnp.where(wide < CP, grad_scale, mean_scale)
    f_zlo = copy(ffull.at[place], ffull.at[place], s_fa.at[0], r_fa.at[0], at_zlo)
    f_zlo.start()
    gx_copies = []
    for j in range(1, 4):
        piece = gfull.at[place, row8]
        gx_copies.append(copy(piece, piece, s_ga.at[j], r_ga.at[x], at_x(j)))
        gx_copies[-1].start()

    own = pacc[tile_of(z, 64)]
    for j in range(1, 8):
        slot = (z + j) % 8
        wait_in(rpz.at[slot], r_pz, slot, s_pz.at[0])
        own = own + rpz[slot]
    base16 = core * 256 + x * 64 + y * 16
    tile = tile_of(z, base16)
    proj_out[tile] = own * grad_scale
    pa_z = []
    for j in range(1, 8):
        piece = proj_out.at[tile]
        pa_z.append(copy(piece, piece, s_pa.at[j], r_pa.at[z], at_z(j)))
        pa_z[-1].start()

    pair = pl.ds(pl.multiple_of(core * 8 + y * 2, 2), 2)
    other_place = core * 8 + y * 2 + (1 - zlo)
    wait_in(ffull.at[other_place], r_fa, 0, s_fa.at[0])
    f_y = []
    for j in range(1, 4):
        f_y.append(copy(ffull.at[pair], ffull.at[pair], s_fa.at[j], r_fa.at[1 + y], at_y(j)))
        f_y[-1].start()
    for j in range(1, 4):
        slot = (x + j) % 4
        wait_in(gfull.at[place, pl.ds(pl.multiple_of(slot * 8, 8), 8)], r_ga, slot, s_ga.at[0])
    g_zlo = copy(gfull.at[place], gfull.at[place], s_ga.at[4], r_ga.at[4], at_zlo)
    g_zlo.start()

    for j in range(1, 8):
        slot = (z + j) % 8
        wait_in(proj_out.at[tile_of(slot, base16)], r_pa, slot, s_pa.at[0])
    pa_y = []
    for j in range(1, 4):
        piece = proj_out.at[pl.ds(pl.multiple_of(base16, 16), 16)]
        pa_y.append(copy(piece, piece, s_pa.at[8 + j], r_pa.at[8 + y], at_y(j)))
        pa_y[-1].start()

    wait_in(gfull.at[other_place], r_ga, 4, s_ga.at[0])
    g_y = []
    for j in range(1, 4):
        g_y.append(copy(gfull.at[pair], gfull.at[pair], s_ga.at[5 + j], r_ga.at[5 + y], at_y(j)))
        g_y[-1].start()

    half8 = pl.ds(pl.multiple_of(core * 8, 8), 8)
    other8 = pl.ds(pl.multiple_of((1 - core) * 8, 8), 8)
    for j in range(1, 4):
        slot = (y + j) % 4
        wait_in(ffull.at[pl.ds(pl.multiple_of(core * 8 + slot * 2, 2), 2)], r_fa, 1 + slot, s_fa.at[0])
    f_core = copy(ffull.at[half8], ffull.at[half8], s_fa.at[5], r_fa.at[5], at_core)
    f_core.start()

    base64 = core * 256 + x * 64
    for j in range(1, 4):
        slot = (y + j) % 4
        piece = proj_out.at[pl.ds(pl.multiple_of(base64 + slot * 16, 16), 16)]
        wait_in(piece, r_pa, 8 + slot, s_pa.at[0])
    pa_x = []
    for j in range(1, 4):
        piece = proj_out.at[pl.ds(pl.multiple_of(base64, 64), 64)]
        pa_x.append(copy(piece, piece, s_pa.at[12 + j], r_pa.at[12 + x], at_x(j)))
        pa_x[-1].start()

    for j in range(1, 4):
        slot = (y + j) % 4
        wait_in(gfull.at[pl.ds(pl.multiple_of(core * 8 + slot * 2, 2), 2)], r_ga, 5 + slot, s_ga.at[0])
    g_core = copy(gfull.at[half8], gfull.at[half8], s_ga.at[9], r_ga.at[9], at_core)
    g_core.start()

    for j in range(1, 4):
        slot = (x + j) % 4
        piece = proj_out.at[pl.ds(pl.multiple_of(core * 256 + slot * 64, 64), 64)]
        wait_in(piece, r_pa, 12 + slot, s_pa.at[0])
    piece = proj_out.at[pl.ds(near, 256)]
    pa_core = copy(piece, piece, s_pa.at[16], r_pa.at[16], at_core)
    pa_core.start()

    wait_in(ffull.at[other8], r_fa, 5, s_fa.at[0])
    for s in range(6):
        block = slot_ref[owner, s]
        which = jnp.maximum(block, 0)
        group = which // 3
        rows = ffull[(group % 2) * 8 + group // 2, which % 3]
        live = jnp.where(block >= 0, 1.0, 0.0).astype(F32)
        fact_out[s] = (rows * live)[0:6, 0:CP]

    wait_in(gfull.at[other8], r_ga, 9, s_ga.at[0])
    for g in range(GROUPS):
        rows = gfull[(g % 2) * 8 + g // 2]
        group_out[g] = rows.T[0:CP, :]
        outf_out[g] = rows[:, CP:CP + GW]

    wait_in(proj_out.at[pl.ds(far, 256)], r_pa, 16, s_pa.at[0])

    def sent(j, carry):
        x_copy(j).wait_send()
        g_copy(j).wait_send()
        return carry

    lax.fori_loop(1, N_OWNER, sent, 0)
    core_copy.wait_send()
    for copied in fg_copies + zh_copies + pz_copies + gx_copies + pa_z + f_y + pa_y + g_y + pa_x:
        copied.wait_send()
    for copied in (f_zlo, g_zlo, f_core, g_core, pa_core):
        copied.wait_send()


def per_device(activations, out_grad, group_weight, proj_weight, bn_gain, bn_shift, slot_block):
    rows = activations.shape[0] * activations.shape[1] * activations.shape[2]
    total_rows = rows * N_OWNER * N_DP
    grad_scale = 1.0 / math.sqrt(total_rows)
    mean_scale = 1.0 / total_rows
    vmem = pl.BlockSpec(memory_space=pltpu.VMEM)
    dma = pltpu.SemaphoreType.DMA
    return pl.pallas_call(
        functools.partial(kernel, grad_scale, mean_scale),
        out_shape=(
            jax.ShapeDtypeStruct((GROUPS, CP, GW), F32),
            jax.ShapeDtypeStruct((512, 512), F32),
            jax.ShapeDtypeStruct((GROUPS, GW, GW), F32),
            jax.ShapeDtypeStruct((6, 6, CP), F32),
        ),
        in_specs=[pl.BlockSpec(memory_space=pltpu.SMEM)] + [vmem] * 6,
        out_specs=(vmem,) * 4,
        scratch_shapes=[
            pltpu.VMEM((GROUPS, GW, 128), F32),
            pltpu.VMEM((GROUPS, GW, 128), F32),
            pltpu.VMEM((GROUPS, GW, 128), F32),
            pltpu.VMEM((GROUPS, GW, 128), F32),
            pltpu.VMEM((GROUPS, CP, 128), BF16),
            pltpu.VMEM((384, 2048), BF16),
            pltpu.VMEM((320, 384), F32),
            pltpu.VMEM((512, 512), F32),
            pltpu.VMEM((256, 512), F32),
            pltpu.VMEM((256, 512), F32),
            pltpu.VMEM((4, 64, 512), F32),
            pltpu.VMEM((4, 16, 512), F32),
            pltpu.VMEM((8, 8, 128), F32),
            pltpu.VMEM((4, 13, 8, 384), F32),
            pltpu.VMEM((4, 13, 8, 384), F32),
            pltpu.VMEM((4, 4, 8, 384), F32),
            pltpu.VMEM((4, 4, 8, 384), F32),
            pltpu.VMEM((GROUPS, GW, 384), F32),
            pltpu.VMEM((GROUPS, 3, 8, 384), F32),
            pltpu.SemaphoreType.REGULAR,
            dma((16,)), dma((16,)), dma((16,)), dma((16,)),
            dma, dma,
            dma((4,)), dma((4,)), dma((4,)), dma((4,)), dma((8,)), dma((8,)),
            dma((4,)), dma((4,)), dma((4,)), dma((4,)),
            dma((10,)), dma((10,)), dma((6,)), dma((6,)), dma((17,)), dma((17,)),
        ],
        compiler_params=pltpu.CompilerParams(
            collective_id=0, has_side_effects=True, vmem_limit_bytes=48 * 1024 * 1024
        ),
    )(
        slot_block,
        activations.reshape(rows, 512),
        out_grad.reshape(rows, 512),
        group_weight,
        proj_weight,
        bn_gain.reshape(1, 512),
        bn_shift.reshape(1, 512),
    )


def solution(mesh):
    placed = (
        P(("owner", "dp"), None, None, None),
        P(("owner", "dp"), None, None, None),
        P(),
        P(),
        P(),
        P(),
        P(),
    )
    return jax.shard_map(
        per_device,
        mesh=mesh,
        in_specs=placed,
        out_specs=(P(), P(), P(), P("owner", "dp", None)),
        check_vma=False,
    )
```

time: 613 us -> 72.1 us (0.12); the launches traced: 602 us -> 71.8 us
  waiting for transfers between devices: 518 us -> 0 us
  Pallas kernels: 0 us -> 57.3 us
  local copies, waits for them, and re-layouts: 37.9 us -> 13.8 us
  other arithmetic: 22 us -> 0 us
  between operations: 16.3 us -> 0.67 us
  matrix products: 8.09 us -> 0 us
    psum x1 -> x0, waiting for transfers between devices: 204 us -> none  [per_device(): lax.psum((group_part, proj_part, out_part), ('owner', 'dp'))]
    reduce_scatter x1 -> x0, waiting for transfers between devices: 159 us -> none  [per_device(): owned = lax.psum_scatter(slotted, 'owner', scatter_dimension=0, tiled=True)]
    unnamed x4 -> x0, waiting for transfers between devices: 155 us -> none
    pallas_call x0 -> x1, Pallas kernels: none -> 57.3 us  [per_device(): pl.pallas_call(functools.partial(kernel, grad_scale, mean_scale), out_sha...]
    mul x5 -> x0, other arithmetic: 20.6 us -> none  [the longest x1 13 us: pick_slots(): return picked * (flat_slots >= 0).astype(jnp.float32)[:, None, None]]
    gather x1 -> x0, local copies, waits for them, and re-layouts: 12.4 us -> none  [pick_slots(): jnp.take(factor_blocks, jnp.clip(flat_slots, 0, factor_blocks.shape[0] -...]
    another operation x2 -> x0, local copies, waits for them, and re-layouts: 11.2 us -> none  [per_device(): patches = jnp.stack(shifted, axis=4).reshape(row_count, groups, patch_len)]
    reshape x4 -> x0, local copies, waits for them, and re-layouts: 10.5 us -> none  [the longest x2 9.86 us: per_device(): patches = jnp.stack(shifted, axis=4).reshape(row_count, groups, patch_len)]
  transfers between devices with their start and end apart: 3 -> 0, of which waited for: 3 -> 0; matrix products, arithmetic and copies ran while one was open for 2% -> 0% of each run, Pallas kernels for 0% -> 0%
where the time goes in v1:
time: 72.1 us; the launch traced here: 71.8 us
  Pallas kernels  57.3 us (79%)
  local copies, waits for them, and re-layouts  13.8 us (19%)
    pallas_call x1, Pallas kernels, per_device(): pl.pallas_call(functools.partial(kernel, grad_scale, mean_scale), out_sha...  57.3 us
    unnamed x25, local copies, waits for them, and re-layouts  12.1 us
    pallas_call x1, local copies, waits for them, and re-layouts, per_device(): pl.pallas_call(functools.partial(kernel, grad_scale, mean_scale), out_sha...  1.73 us

profile of v1, /device:TPU:1, one launch (start us, length us, event | category | flops | bytes accessed | tf_op | source)
XLA Modules:
  0.0 71.8 jit_solution(10578486469860200917)
XLA Ops:
  0.6 0.8 %copy.11.slot_ref = s32[16,6]{1,0:T(8,128)S(1)} copy(s32[16,6]{0,1:T(8,128)} %param.13) | data formatting | bytes 768 | tf_op args[6]
  1.4 1.5 %copy.12.gw_ref = bf16[16,288,32]{2,1,0:T(8,128)(2,1)S(1)} copy(bf16[16,288,32]{1,2,0:T(8,128)(2,1)} %param.9) | data formatting | bytes 589824 | tf_op args[2]
  2.9 0.0 copy-start.2
  2.9 1.0 %copy-done.2 = bf16[512,512]{1,0:T(8,128)(2,1)S(1)} copy-done((bf16[512,512]{1,0:T(8,128)(2,1)S(1)}, bf16[512,512]{1,0:T(8,128)(2,1)}, u32[]{:S(2)}) %copy-start.2) | copy-done | bytes 524312
  4.0 0.0 copy-start.4
  4.0 0.9 %copy-done.4 = bf16[2,8,8,512]{3,2,1,0:T(8,128)(2,1)S(1)} copy-done((bf16[2,8,8,512]{3,2,1,0:T(8,128)(2,1)S(1)}, bf16[2,8,8,512]{3,2,1,0:T(8,128)(2,1)}, u32[]{:S(2)}) %copy-start.4) | copy-done | bytes 131096
  4.9 0.0 copy-start.5
  4.9 0.9 %copy-done.5 = bf16[2,8,8,512]{3,2,1,0:T(8,128)(2,1)S(1)} copy-done((bf16[2,8,8,512]{3,2,1,0:T(8,128)(2,1)S(1)}, bf16[2,8,8,512]{3,2,1,0:T(8,128)(2,1)}, u32[]{:S(2)}) %copy-start.5) | copy-done | bytes 131096
  5.8 0.0 copy-start.8
  5.8 0.7 copy-done.8
  6.5 0.7 copy-done.9
  7.1 57.3 %shard_map.102 = (f32[16,288,32]{2,1,0:T(8,128)S(1)}, f32[512,512]{1,0:T(8,128)S(1)}, f32[16,32,32]{2,1,0:T(8,128)S(1)}, f32[6,6,288]{2,1,0:T(8,128)S(1)}) custom-call(s32[16,6]{1,0:T(8,128)S(1)} %copy.11.slot_ref, bf16[128,512]{1,0:T(8,128)(2,1)S(1)} %bitcast.4, bf16[128,512]{1,0:T(8,128)(2,1)S(1)} %bitcast.5, bf16[16,288,32]{2,1,0:T(8,128)(2,1)S(1)} %copy.12.gw_ref, ...), custom_call_target="tpu_custom_call" | custom-call | tf_op jit(solution)/shard_map/pallas_call | solution.py:360
  64.4 0.0 copy-start
  64.4 1.0 %copy-done = f32[512,512]{1,0:T(8,128)} copy-done((f32[512,512]{1,0:T(8,128)}, f32[512,512]{1,0:T(8,128)S(1)}, u32[]{:S(2)}) %copy-start) | copy-done | bytes 1048600
  65.4 0.0 copy-start.3
  65.4 0.7 copy-done.3
  66.1 0.0 copy-start.6
  66.1 0.6 copy-done.6
  66.7 1.7 %copy.13 = f32[16,288,32]{1,2,0:T(8,128)} copy(f32[16,288,32]{2,1,0:T(8,128)S(1)} %get-tuple-element.4) | data formatting | bytes 1179648 | tf_op jit(solution)/shard_map/pallas_call | solution.py:360
  68.5 0.0 copy-done.1
  68.5 1.0 %copy.17 = f32[512,512]{1,0:T(8,128)} copy(f32[512,512]{1,0:T(8,128)S(1)} %copy-done.1) | data formatting | bytes 2097152
  69.5 1.7 %copy.18 = f32[16,32,32]{2,1,0:T(8,128)} copy(f32[16,32,32]{2,1,0:T(8,128)} %copy-done.3) | data formatting | bytes 131072
  71.1 0.0 copy-done.7
  71.1 0.6 copy.19
  (3 shorter events, 0.0 us)
Async XLA Ops:
  2.9 1.0 %copy-start.2 = (bf16[512,512]{1,0:T(8,128)(2,1)S(1)}, bf16[512,512]{1,0:T(8,128)(2,1)}, u32[]{:S(2)}) copy-start(bf16[512,512]{1,0:T(8,128)(2,1)} %pw_ref.1) | copy-start | bytes 1572868
  4.0 0.9 %copy-start.4 = (bf16[2,8,8,512]{3,2,1,0:T(8,128)(2,1)S(1)}, bf16[2,8,8,512]{3,2,1,0:T(8,128)(2,1)}, u32[]{:S(2)}) copy-start(bf16[2,8,8,512]{3,2,1,0:T(8,128)(2,1)} %param.7) | copy-start | bytes 393220
  4.9 0.9 %copy-start.5 = (bf16[2,8,8,512]{3,2,1,0:T(8,128)(2,1)S(1)}, bf16[2,8,8,512]{3,2,1,0:T(8,128)(2,1)}, u32[]{:S(2)}) copy-start(bf16[2,8,8,512]{3,2,1,0:T(8,128)(2,1)} %param.8) | copy-start | bytes 393220
  5.8 0.7 copy-start.8
  6.5 0.7 copy-start.9
  64.4 1.0 %copy-start = (f32[512,512]{1,0:T(8,128)}, f32[512,512]{1,0:T(8,128)S(1)}, u32[]{:S(2)}) copy-start(f32[512,512]{1,0:T(8,128)S(1)} %get-tuple-element.13) | copy-start | bytes 3145732
  65.4 0.7 copy-start.3
  66.1 0.6 copy-start.6
  66.7 1.7 %copy-start.1 = (f32[512,512]{1,0:T(8,128)S(1)}, f32[512,512]{1,0:T(8,128)}, u32[]{:S(2)}) copy-start(f32[512,512]{1,0:T(8,128)} %copy-done) | copy-start | bytes 3145732
  66.7 4.4 %copy-start.7 = (f32[6,6,288]{2,1,0:T(8,128)S(1)}, f32[6,6,288]{2,1,0:T(8,128)}, u32[]{:S(2)}) copy-start(f32[6,6,288]{2,1,0:T(8,128)} %copy-done.6) | copy-start | bytes 124420

commit v2 on v0

v2 whole, which is shorter than its diff:
```python
import functools
import math

import jax
import jax.numpy as jnp
from jax import lax
from jax.experimental import pallas as pl
from jax.experimental.pallas import tpu as pltpu
from jax.sharding import PartitionSpec as P

MESH = pl.DeviceIdType.MESH
F32 = jnp.float32
BF16 = jnp.bfloat16
NT = (((1,), (1,)), ((), ()))
GROUPS, GW, CP = 16, 32, 288
N_OWNER, N_DP = 16, 16
MAIN, REST, FACT = 256, 768, 896
LEFT, RIGHT = slice(0, 256), slice(256, 512)


def shifted_rows(tile, lane, store):
    row = (lane // 8) % 8
    col = lane % 8
    for a in range(3):
        for b in range(3):
            offset = (a - 1) * 8 + (b - 1)
            moved = tile if offset == 0 else pltpu.roll(tile, (-offset) % 128, 1)
            keep = None
            if a == 0:
                keep = row >= 1
            if a == 2:
                keep = row <= 6
            if b == 0:
                keep = (col >= 1) if keep is None else keep & (col >= 1)
            if b == 2:
                keep = (col <= 6) if keep is None else keep & (col <= 6)
            if keep is not None:
                moved = jnp.where(keep, moved, 0.0)
            store(3 * a + b, moved.astype(BF16))


def rows_at(start, size):
    return pl.ds(pl.multiple_of(start, size), size)


class Stage:
    def __init__(self, send, recv, base=0):
        self.send, self.recv, self.base = send, recv, base
        self.sent, self.due = [], []

    def put(self, src, dst, device, here, arrival, there):
        copy = pltpu.make_async_remote_copy(
            src_ref=src, dst_ref=dst, send_sem=self.send.at[self.base + len(self.sent)],
            recv_sem=self.recv.at[self.base + here], device_id=device, device_id_type=MESH,
        )
        copy.start()
        self.sent.append(copy)
        self.due.append(
            pltpu.make_async_remote_copy(
                src_ref=arrival, dst_ref=arrival, send_sem=self.send.at[self.base],
                recv_sem=self.recv.at[self.base + there], device_id=device, device_id_type=MESH,
            )
        )

    def take(self):
        self.due.pop(0).wait_recv()

    def take_all(self):
        while self.due:
            self.take()

    def drain(self):
        while self.sent:
            self.sent.pop(0).wait_send()


def kernel(
    grad_scale, mean_scale,
    x_hbm, u_hbm, gw_hbm, pw_hbm, gain_hbm, shift_hbm,
    gfull, pfull, ffull,
    x_in, u_in, gw_in, pw_in, gain_in, shift_in,
    x_t, g_t, rx, rg, pt, zt, gram, fcat, ppart, rcore, pacc, rp1, pmid, rp2, plast, rpl, rpz,
    f_send, rf, zh_send, rzh, gp_send, rgx, rgz,
    in_sem, sx, rxs, sg, rgs, s_p, r_p, s_f, r_f, s_g, r_g,
):
    loads = [
        pltpu.make_async_copy(src, dst, in_sem.at[i])
        for i, (src, dst) in enumerate(
            ((x_hbm, x_in), (u_hbm, u_in), (gw_hbm, gw_in), (pw_hbm, pw_in), (gain_hbm, gain_in), (shift_hbm, shift_in))
        )
    ]
    for load in loads:
        load.start()

    owner = lax.axis_index("owner")
    dp = lax.axis_index("dp")
    core = owner % 2
    zlo = (owner // 2) % 2
    y = owner // 4
    x = dp % 4
    zhi = dp // 4

    def at_y(j):
        return (((y + j) % 4) * 4 + zlo * 2 + core, dp)

    def at_x(j):
        return (owner, zhi * 4 + (x + j) % 4)

    def at_zhi(j):
        return (owner, ((zhi + j) % 4) * 4 + x)

    at_zlo = (y * 4 + (1 - zlo) * 2 + core, dp)
    at_core = (y * 4 + zlo * 2 + (1 - core), dp)

    barrier = pltpu.get_barrier_semaphore()
    for j in range(1, N_OWNER):
        pl.semaphore_signal(barrier, inc=1, device_id=((owner + j) % N_OWNER, dp), device_id_type=MESH)
    for j in range(1, 4):
        pl.semaphore_signal(barrier, inc=1, device_id=at_x(j), device_id_type=MESH)
        pl.semaphore_signal(barrier, inc=1, device_id=at_zhi(j), device_id_type=MESH)

    loads[0].wait()
    x_rows = x_in[...].astype(F32).T
    x_t[...] = x_rows.reshape(GROUPS, GW, 128)
    pl.semaphore_wait(barrier, 21)

    def exchange(own, landed, send, recv):
        stage = Stage(send, recv)
        for j in range(1, N_OWNER):
            there = (owner + j) % N_OWNER
            source = (owner + N_OWNER - j) % N_OWNER
            stage.put(own.at[there], landed.at[owner], (there, dp), owner, landed.at[source], source)
        return stage

    x_stage = exchange(x_t, rx, sx, rxs)
    stages = [x_stage]
    rx[owner] = x_t[owner]

    lane = lax.broadcasted_iota(jnp.int32, (GW, 128), 1)
    for load in loads[1:]:
        load.wait()
    gain_col = jnp.broadcast_to(gain_in[...], (128, 512)).T
    shift_col = jnp.broadcast_to(shift_in[...], (128, 512)).T
    upstream = u_in[...]
    back = lax.dot_general(pw_in[...], upstream, NT, preferred_element_type=F32)
    conv = []
    for g in range(GROUPS):
        def put(s, value, g=g):
            pt[g, s * GW:(s + 1) * GW, :] = value

        shifted_rows(x_rows[g * GW:(g + 1) * GW, :], lane, put)
        conv.append(jnp.dot(gw_in[g], pt[g], preferred_element_type=F32))
    preact = jnp.concatenate(conv, axis=0) * gain_col + shift_col
    grad = jnp.where(preact > 0.0, back * gain_col, 0.0).astype(BF16).astype(F32)
    g_t[...] = grad.reshape(GROUPS, GW, 128)
    g_stage = exchange(g_t, rg, sg, rgs)
    stages.append(g_stage)
    rg[owner] = g_t[owner]

    hidden = jnp.maximum(preact, 0.0).astype(BF16)
    ppart[...] = jnp.dot(hidden, upstream, preferred_element_type=F32)
    far, near = rows_at((1 - core) * 256, 256), rows_at(core * 256, 256)
    pc = Stage(s_p, r_p, 0)
    pc.put(ppart.at[far], rcore, at_core, 0, rcore, 0)
    stages.append(pc)

    pc.take()
    pacc[...] = ppart[near, :] + rcore[...]
    px, py = Stage(s_p, r_p, 1), Stage(s_p, r_p, 5)
    stages += [px, py]
    for j in range(1, 4):
        slot = (x + j) % 4
        px.put(pacc.at[rows_at(slot * 64, 64), LEFT], rp1.at[x, :, LEFT], at_x(j), x, rp1.at[slot, :, LEFT], slot)
        slot = (y + j) % 4
        py.put(pacc.at[rows_at(slot * 64, 64), RIGHT], rp1.at[y, :, RIGHT], at_y(j), y, rp1.at[slot, :, RIGHT], slot)

    zt[320:384, :] = jnp.zeros((64, 2048), BF16)
    zh_send[:, 6:8, :] = jnp.zeros((4, 2, FACT), F32)
    for j in range(N_OWNER):
        source = (owner + N_OWNER - j) % N_OWNER
        if j:
            x_stage.take()
        lanes = slice(j * 128, (j + 1) * 128)

        def put_z(s, value, lanes=lanes):
            zt[s * GW:(s + 1) * GW, lanes] = value

        shifted_rows(rx[source], lane, put_z)

    gram[...] = lax.dot_general(zt[0:CP, :], zt[0:CP, :], NT, preferred_element_type=F32)
    for a in range(3):
        fcat[:, a * MAIN:(a + 1) * MAIN] = gram[a * 96:a * 96 + 96, 0:MAIN]
        fcat[:, REST + a * 32:REST + a * 32 + 32] = gram[a * 96:a * 96 + 96, MAIN:CP]
    fcat[:, REST + 96:FACT] = jnp.zeros((96, 32), F32)
    for xx in range(4):
        for zz in range(4):
            at = (zz * 4 + xx) * 6
            f_send[xx, zz * 6:zz * 6 + 6, :] = fcat[at:at + 6, :]
    fx = Stage(s_f, r_f, 0)
    stages.append(fx)
    for j in range(1, 4):
        slot = (x + j) % 4
        fx.put(f_send.at[slot], rf.at[x], at_x(j), x, rf.at[slot], slot)

    for j in range(N_OWNER):
        source = (owner + N_OWNER - j) % N_OWNER
        if j:
            g_stage.take()
        zt[CP:CP + GW, j * 128:(j + 1) * 128] = rg[source].astype(BF16)
    part = lax.dot_general(zt[CP:CP + GW, :], zt[...], NT, preferred_element_type=F32)
    gp_send[...] = part.reshape(4, 8, 384)
    gpx = Stage(s_g, r_g, 0)
    stages.append(gpx)
    for j in range(1, 4):
        slot = (x + j) % 4
        gpx.put(gp_send.at[slot], rgx.at[x], at_x(j), x, rgx.at[slot], slot)

    left = pacc[rows_at(x * 64, 64), LEFT]
    right = pacc[rows_at(y * 64, 64), RIGHT]
    for j in range(1, 4):
        px.take()
        left = left + rp1[(x + j) % 4, :, LEFT]
        py.take()
        right = right + rp1[(y + j) % 4, :, RIGHT]
    pmid[:, LEFT] = left
    pmid[:, RIGHT] = right
    py2, px2 = Stage(s_p, r_p, 9), Stage(s_p, r_p, 13)
    stages += [py2, px2]
    for j in range(1, 4):
        slot = (y + j) % 4
        py2.put(pmid.at[rows_at(slot * 16, 16), LEFT], rp2.at[y, :, LEFT], at_y(j), y, rp2.at[slot, :, LEFT], slot)
        slot = (x + j) % 4
        px2.put(pmid.at[rows_at(slot * 16, 16), RIGHT], rp2.at[x, :, RIGHT], at_x(j), x, rp2.at[slot, :, RIGHT], slot)

    fx.take_all()
    rf[x] = f_send[x]
    summed = (rf[0] + rf[1]) + (rf[2] + rf[3])
    for zz in range(4):
        zh_send[zz, 0:6, :] = summed[zz * 6:zz * 6 + 6]
    fz = Stage(s_f, r_f, 4)
    stages.append(fz)
    for j in range(1, 4):
        slot = (zhi + j) % 4
        fz.put(zh_send.at[slot], rzh.at[zhi], at_zhi(j), zhi, rzh.at[slot], slot)
    gpx.take_all()
    rgx[x] = gp_send[x]
    rgz[zhi] = (rgx[0] + rgx[1]) + (rgx[2] + rgx[3])
    gpz = Stage(s_g, r_g, 4)
    stages.append(gpz)
    for j in range(1, 4):
        slot = (zhi + j) % 4
        gpz.put(rgz.at[zhi], rgz.at[zhi], at_zhi(j), zhi, rgz.at[slot], slot)

    left = pmid[rows_at(y * 16, 16), LEFT]
    right = pmid[rows_at(x * 16, 16), RIGHT]
    for j in range(1, 4):
        py2.take()
        left = left + rp2[(y + j) % 4, :, LEFT]
        px2.take()
        right = right + rp2[(x + j) % 4, :, RIGHT]
    plast[:, LEFT] = left
    plast[:, RIGHT] = right
    plo = Stage(s_p, r_p, 17)
    stages.append(plo)
    plo.put(plast.at[rows_at((1 - zlo) * 8, 8)], rpl, at_zlo, 0, rpl, 0)
    plo.take()
    rpz[zhi] = plast[rows_at(zlo * 8, 8), :] + rpl[...]
    pz = Stage(s_p, r_p, 18)
    stages.append(pz)
    for j in range(1, 4):
        slot = (zhi + j) % 4
        pz.put(rpz.at[zhi], rpz.at[zhi], at_zhi(j), zhi, rpz.at[slot], slot)

    fz.take_all()
    rzh[zhi] = zh_send[zhi]
    place = core * 8 + y * 2 + zlo
    other_place = core * 8 + y * 2 + (1 - zlo)
    pair = rows_at(core * 8 + y * 2, 2)
    half8, other8 = rows_at(core * 8, 8), rows_at((1 - core) * 8, 8)
    row8 = rows_at(x * 8, 8)
    ffull[place] = ((rzh[0] + rzh[1]) + (rzh[2] + rzh[3])) * mean_scale
    fl = Stage(s_f, r_f, 8)
    stages.append(fl)
    fl.put(ffull.at[place], ffull.at[place], at_zlo, 0, ffull.at[other_place], 0)
    gpz.take_all()
    wide = lax.broadcasted_iota(jnp.int32, (8, 384), 1)
    total = (rgz[0] + rgz[1]) + (rgz[2] + rgz[3])
    gfull[place, row8, :] = total * jnp.where(wide < CP, grad_scale, mean_scale)
    gl = Stage(s_g, r_g, 8)
    stages.append(gl)
    piece = gfull.at[place, row8]
    gl.put(piece, piece, at_zlo, 0, gfull.at[other_place, row8], 0)
    fl.take()
    fy = Stage(s_f, r_f, 9)
    stages.append(fy)
    for j in range(1, 4):
        slot = (y + j) % 4
        fy.put(ffull.at[pair], ffull.at[pair], at_y(j), y, ffull.at[rows_at(core * 8 + slot * 2, 2)], slot)
    gl.take()
    gy = Stage(s_g, r_g, 9)
    stages.append(gy)
    for j in range(1, 4):
        slot = (y + j) % 4
        piece = gfull.at[pair, row8]
        gy.put(piece, piece, at_y(j), y, gfull.at[rows_at(core * 8 + slot * 2, 2), row8], slot)

    pz.take_all()
    total = ((rpz[0] + rpz[1]) + (rpz[2] + rpz[3])) * grad_scale
    base_l = core * 256 + x * 64
    base_r = core * 256 + y * 64
    fin_l, fin_r = rows_at(base_l + y * 16 + zlo * 8, 8), rows_at(base_r + x * 16 + zlo * 8, 8)
    oth_l, oth_r = rows_at(base_l + y * 16 + (1 - zlo) * 8, 8), rows_at(base_r + x * 16 + (1 - zlo) * 8, 8)
    pfull[fin_l, LEFT] = total[:, LEFT]
    pfull[fin_r, RIGHT] = total[:, RIGHT]
    pal, par = Stage(s_p, r_p, 22), Stage(s_p, r_p, 23)
    stages += [pal, par]
    pal.put(pfull.at[fin_l, LEFT], pfull.at[fin_l, LEFT], at_zlo, 0, pfull.at[oth_l, LEFT], 0)
    par.put(pfull.at[fin_r, RIGHT], pfull.at[fin_r, RIGHT], at_zlo, 0, pfull.at[oth_r, RIGHT], 0)
    pal.take()
    par.take()
    pay, pax = Stage(s_p, r_p, 24), Stage(s_p, r_p, 28)
    stages += [pay, pax]
    for j in range(1, 4):
        slot = (y + j) % 4
        piece = pfull.at[rows_at(base_l + y * 16, 16), LEFT]
        pay.put(piece, piece, at_y(j), y, pfull.at[rows_at(base_l + slot * 16, 16), LEFT], slot)
        slot = (x + j) % 4
        piece = pfull.at[rows_at(base_r + x * 16, 16), RIGHT]
        pax.put(piece, piece, at_x(j), x, pfull.at[rows_at(base_r + slot * 16, 16), RIGHT], slot)

    gy.take_all()
    gx = Stage(s_g, r_g, 13)
    stages.append(gx)
    for j in range(1, 4):
        slot = (x + j) % 4
        piece = gfull.at[half8, row8]
        gx.put(piece, piece, at_x(j), x, gfull.at[half8, rows_at(slot * 8, 8)], slot)
    pay.take_all()
    pax2 = Stage(s_p, r_p, 32)
    stages.append(pax2)
    for j in range(1, 4):
        slot = (x + j) % 4
        piece = pfull.at[rows_at(base_l, 64), LEFT]
        pax2.put(piece, piece, at_x(j), x, pfull.at[rows_at(core * 256 + slot * 64, 64), LEFT], slot)
    pax.take_all()
    pay2 = Stage(s_p, r_p, 36)
    stages.append(pay2)
    for j in range(1, 4):
        slot = (y + j) % 4
        piece = pfull.at[rows_at(base_r, 64), RIGHT]
        pay2.put(piece, piece, at_y(j), y, pfull.at[rows_at(core * 256 + slot * 64, 64), RIGHT], slot)

    fy.take_all()
    fc, gc, pcl, pcr = Stage(s_f, r_f, 13), Stage(s_g, r_g, 17), Stage(s_p, r_p, 40), Stage(s_p, r_p, 41)
    stages += [fc, gc, pcl, pcr]
    fc.put(ffull.at[half8], ffull.at[half8], at_core, 0, ffull.at[other8], 0)
    gx.take_all()
    gc.put(gfull.at[half8], gfull.at[half8], at_core, 0, gfull.at[other8], 0)
    pay2.take_all()
    pcr.put(pfull.at[near, RIGHT], pfull.at[near, RIGHT], at_core, 0, pfull.at[far, RIGHT], 0)
    pax2.take_all()
    pcl.put(pfull.at[near, LEFT], pfull.at[near, LEFT], at_core, 0, pfull.at[far, LEFT], 0)
    for stage in stages:
        stage.take_all()
    for stage in stages:
        stage.drain()


def finish_kernel(slot_ref, gfull, pfull, ffull, group_out, proj_out, outf_out, fact_out, gs, os, fs, sem):
    owner = lax.axis_index("owner")
    copies = [pltpu.make_async_copy(pfull, proj_out, sem.at[0])]
    copies[0].start()
    for g in range(GROUPS):
        q = (g % 2) * 8 + g // 2
        gs[g] = gfull[q, :, 0:CP]
        os[g] = gfull[q, :, CP:CP + GW]
    copies.append(pltpu.make_async_copy(gs, group_out, sem.at[1]))
    copies.append(pltpu.make_async_copy(os, outf_out, sem.at[2]))
    copies[1].start()
    copies[2].start()
    for s in range(6):
        block = slot_ref[s, owner]
        which = jnp.maximum(block, 0)
        group, a = which // 3, which % 3
        rows = ffull[(group % 2) * 8 + group // 2]
        live = jnp.where(block >= 0, 1.0, 0.0).astype(F32)
        pick = [rows[:, k * MAIN:(k + 1) * MAIN] for k in range(3)]
        rest = [rows[:, REST + k * 32:REST + k * 32 + 32] for k in range(3)]
        for lanes, parts in ((slice(0, MAIN), pick), (slice(MAIN, CP), rest)):
            value = jnp.where(a == 0, parts[0], jnp.where(a == 1, parts[1], parts[2])) * live
            fs[s, :, lanes] = value[0:6]
    copies.append(pltpu.make_async_copy(fs, fact_out, sem.at[3]))
    copies[3].start()
    for copy in copies:
        copy.wait()


def per_device(activations, out_grad, group_weight, proj_weight, bn_gain, bn_shift, slot_block):
    rows = activations.shape[0] * activations.shape[1] * activations.shape[2]
    total_rows = rows * N_OWNER * N_DP
    grad_scale = 1.0 / math.sqrt(total_rows)
    mean_scale = 1.0 / total_rows
    vmem = pl.BlockSpec(memory_space=pltpu.VMEM)
    hbm = pl.BlockSpec(memory_space=pltpu.HBM)
    dma = pltpu.SemaphoreType.DMA
    full = pl.pallas_call(
        functools.partial(kernel, grad_scale, mean_scale),
        out_shape=(
            jax.ShapeDtypeStruct((GROUPS, GW, 384), F32),
            jax.ShapeDtypeStruct((512, 512), F32),
            jax.ShapeDtypeStruct((GROUPS, 8, FACT), F32),
        ),
        in_specs=[hbm] * 6,
        out_specs=(vmem,) * 3,
        scratch_shapes=[
            pltpu.VMEM((rows, 512), BF16),
            pltpu.VMEM((rows, 512), BF16),
            pltpu.VMEM((GROUPS, GW, CP), BF16),
            pltpu.VMEM((512, 512), BF16),
            pltpu.VMEM((1, 512), F32),
            pltpu.VMEM((1, 512), F32),
            pltpu.VMEM((GROUPS, GW, 128), F32),
            pltpu.VMEM((GROUPS, GW, 128), F32),
            pltpu.VMEM((GROUPS, GW, 128), F32),
            pltpu.VMEM((GROUPS, GW, 128), F32),
            pltpu.VMEM((GROUPS, CP, 128), BF16),
            pltpu.VMEM((384, 2048), BF16),
            pltpu.VMEM((CP, CP), F32),
            pltpu.VMEM((96, FACT), F32),
            pltpu.VMEM((512, 512), F32),
            pltpu.VMEM((256, 512), F32),
            pltpu.VMEM((256, 512), F32),
            pltpu.VMEM((4, 64, 512), F32),
            pltpu.VMEM((64, 512), F32),
            pltpu.VMEM((4, 16, 512), F32),
            pltpu.VMEM((16, 512), F32),
            pltpu.VMEM((8, 512), F32),
            pltpu.VMEM((4, 8, 512), F32),
            pltpu.VMEM((4, 24, FACT), F32),
            pltpu.VMEM((4, 24, FACT), F32),
            pltpu.VMEM((4, 8, FACT), F32),
            pltpu.VMEM((4, 8, FACT), F32),
            pltpu.VMEM((4, 8, 384), F32),
            pltpu.VMEM((4, 8, 384), F32),
            pltpu.VMEM((4, 8, 384), F32),
            dma((6,)),
            dma((16,)), dma((16,)), dma((16,)), dma((16,)),
            dma((42,)), dma((42,)), dma((14,)), dma((14,)), dma((18,)), dma((18,)),
        ],
        compiler_params=pltpu.CompilerParams(
            collective_id=0, has_side_effects=True
        ),
    )(
        activations.reshape(rows, 512),
        out_grad.reshape(rows, 512),
        jnp.swapaxes(group_weight, 1, 2),
        proj_weight,
        bn_gain.reshape(1, 512),
        bn_shift.reshape(1, 512),
    )
    group_grad, proj_grad, out_factor, owned = pl.pallas_call(
        finish_kernel,
        out_shape=(
            jax.ShapeDtypeStruct((GROUPS, GW, CP), F32),
            jax.ShapeDtypeStruct((512, 512), F32),
            jax.ShapeDtypeStruct((GROUPS, GW, GW), F32),
            jax.ShapeDtypeStruct((6, 6, CP), F32),
        ),
        in_specs=[pl.BlockSpec(memory_space=pltpu.SMEM)] + [vmem] * 3,
        out_specs=(hbm,) * 4,
        scratch_shapes=[
            pltpu.VMEM((GROUPS, GW, CP), F32),
            pltpu.VMEM((GROUPS, GW, GW), F32),
            pltpu.VMEM((6, 6, CP), F32),
            dma((4,)),
        ],
    )(slot_block.T, *full)
    return jnp.swapaxes(group_grad, 1, 2), proj_grad, out_factor, owned


def solution(mesh):
    placed = (
        P(("owner", "dp"), None, None, None),
        P(("owner", "dp"), None, None, None),
        P(),
        P(),
        P(),
        P(),
        P(),
    )
    return jax.shard_map(
        per_device,
        mesh=mesh,
        in_specs=placed,
        out_specs=(P(), P(), P(), P("owner", "dp", None)),
        check_vma=False,
    )
```

time: 613 us -> 55.9 us (0.09); the launches traced: 602 us -> 55.8 us
  waiting for transfers between devices: 518 us -> 0 us
  Pallas kernels: 0 us -> 55.1 us
  local copies, waits for them, and re-layouts: 37.9 us -> 0 us
  other arithmetic: 22 us -> 0 us
  between operations: 16.3 us -> 0.64 us
  matrix products: 8.09 us -> 0 us
    psum x1 -> x0, waiting for transfers between devices: 204 us -> none  [per_device(): lax.psum((group_part, proj_part, out_part), ('owner', 'dp'))]
    reduce_scatter x1 -> x0, waiting for transfers between devices: 159 us -> none  [per_device(): owned = lax.psum_scatter(slotted, 'owner', scatter_dimension=0, tiled=True)]
    unnamed x4 -> x0, waiting for transfers between devices: 155 us -> none
    pallas_call x0 -> x2, Pallas kernels: none -> 55.1 us  [the longest x1 52.2 us: per_device(): pl.pallas_call(functools.partial(kernel, grad_scale, mean_scale), out_sha...]
    mul x5 -> x0, other arithmetic: 20.6 us -> none  [the longest x1 13 us: pick_slots(): return picked * (flat_slots >= 0).astype(jnp.float32)[:, None, None]]
    gather x1 -> x0, local copies, waits for them, and re-layouts: 12.4 us -> none  [pick_slots(): jnp.take(factor_blocks, jnp.clip(flat_slots, 0, factor_blocks.shape[0] -...]
    another operation x2 -> x0, local copies, waits for them, and re-layouts: 11.2 us -> none  [per_device(): patches = jnp.stack(shifted, axis=4).reshape(row_count, groups, patch_len)]
    reshape x4 -> x0, local copies, waits for them, and re-layouts: 10.5 us -> none  [the longest x2 9.86 us: per_device(): patches = jnp.stack(shifted, axis=4).reshape(row_count, groups, patch_len)]
  transfers between devices with their start and end apart: 3 -> 0, of which waited for: 3 -> 0; matrix products, arithmetic and copies ran while one was open for 2% -> 0% of each run, Pallas kernels for 0% -> 0%
where the time goes in v2:
time: 55.9 us; the launch traced here: 55.8 us
  Pallas kernels  55.1 us (99%)
  between operations  0.64 us (1%)
    pallas_call x1, Pallas kernels, per_device(): pl.pallas_call(functools.partial(kernel, grad_scale, mean_scale), out_sha...  52.2 us
    pallas_call x1, Pallas kernels, per_device(): pl.pallas_call(finish_kernel, out_shape=(jax.ShapeDtypeStruct((GROUPS, GW...  2.94 us

profile of v2, /device:TPU:1, one launch (start us, length us, event | category | flops | bytes accessed | tf_op | source)
XLA Modules:
  0.0 55.8 jit_solution(15395515557892846232)
XLA Ops:
  0.6 52.2 %shard_map.102 = (f32[16,32,384]{2,1,0:T(8,128)}, f32[512,512]{1,0:T(8,128)}, f32[16,8,896]{2,1,0:T(8,128)}) custom-call(bf16[128,512]{1,0:T(8,128)(2,1)} %bitcast.8, bf16[128,512]{1,0:T(8,128)(2,1)} %bitcast.9, bf16[16,32,288]{2,1,0:T(8,128)(2,1)} %bitcast.7, bf16[512,512]{1,0:T(8,128)(2,1)} %pw_hbm.1, f32[1,512]{1,0:T(1,128)} %bitcast.11, f32[1,512]{1,0:T(1,128)} %bitcast.12), custom_call_target="tpu_custom_call" | custom-call | tf_op jit(solution)/shard_map/pallas_call | solution.py:406
  52.8 2.9 %shard_map.103 = (f32[16,32,288]{2,1,0:T(8,128)}, f32[512,512]{1,0:T(8,128)}, f32[16,32,32]{2,1,0:T(8,128)}, f32[6,6,288]{2,1,0:T(8,128)}) custom-call(s32[6,16]{1,0:T(8,128)} %bitcast.10, f32[16,32,384]{2,1,0:T(8,128)} %get-tuple-element.11.gfull, f32[512,512]{1,0:T(8,128)} %get-tuple-element.12.pfull, f32[16,8,896]{2,1,0:T(8,128)} %get-tuple-element.13.ffull), custom_call_target="tpu_custom_call" | custom-call | tf_op jit(solution)/shard_map/pallas_call | solution.py:461
